TPU v7x, 128 devices: a whole 4x4x4 slice. The times are simulated.
128 devices in a mesh: stn: 64 (over x, z, y_lo, core), frq: 2 (over y_hi).
Axes of the slice: x: 4, y: 4 (y_hi: 2, y_lo: 2; y = y_hi * 2 + y_lo), z: 4, core: 2. Of those that a mesh axis runs over, the one named last changes fastest.
Arguments:
- spectra: bfloat16 [512, 2, 8192], P('stn', None, 'frq'), may hold values from -60 to 60, as said below
- pair_bin: int32 [16384, 1], P('stn'), may hold values from 0 to 63; in each aligned block of 256 rows (0 to 255, 256 to 511, ...) at most 10 rows name the same one
- pair_valid: int32 [16384], P('stn'), may hold values 0 or 1
- stack_in: float32 [64, 2048], P('stn', 'frq'), may hold values from -1.5 to 1.5
Outputs:
- stacks: float32 [64, 2048], P('stn', 'frq')
Inputs may be any that keep to these rules, and one draw needn't show every extreme that they name: `spectra`: values have rough magnitudes, differing from bin to bin. `pair_bin`: in the 256 rows of one index of stn no bin is named more than 10 times.
All inputs are finite; a program needn't handle non-finite values. No bound on the sum of `pair_valid` on one device may be relied on, other than what follows from the above.
Results may differ from a plain program's by a relative error of at most 0.008.
Values may be sent and summed in bfloat16 or wider, within the bound.
A program may use at most 64 MiB of HBM per device.

v0:
```python
import math

import jax
import jax.numpy as jnp
from jax import lax
from jax.sharding import PartitionSpec as P

ROUNDS = 4
FREQ = 8192
SAMPLES = 32768
LAGS = 2048
WBLK = 32
LBLK = 512


def passed_along(value, axis, steps):
    count = lax.axis_size(axis)
    pairs = [(source, (source + steps) % count) for source in range(count)]
    return lax.ppermute(value, axis, pairs)


def whiten_band(spectra):
    count = spectra.shape[0]
    width = spectra.shape[2]
    values = spectra.astype(jnp.float32)
    blocks = values.reshape(count, 2, width // WBLK, WBLK)
    power = jnp.mean(blocks * blocks, axis=(1, 3), keepdims=True)
    return (blocks / jnp.sqrt(power + 1e-06)).reshape(count, 2, width).astype(jnp.bfloat16)


def cross_block(own, partner):
    own_f = own.astype(jnp.float32)
    part_f = partner.astype(jnp.float32)
    real_part = (
        own_f[:, 0][:, None, :] * part_f[:, 0][None] + own_f[:, 1][:, None, :] * part_f[:, 1][None]
    )
    imag_part = (
        own_f[:, 1][:, None, :] * part_f[:, 0][None] - own_f[:, 0][:, None, :] * part_f[:, 1][None]
    )
    joined = jnp.concatenate([real_part, imag_part], axis=2)
    return joined.reshape(own.shape[0] * partner.shape[0], -1).astype(jnp.bfloat16)


def lag_table(band_start, count, lag_start, lag_count):
    freq_index = band_start + 1 + lax.iota(jnp.int32, count)
    lag_index = lag_start - LAGS // 2 + lax.iota(jnp.int32, lag_count)
    product = freq_index[:, None] * lag_index[None, :] % SAMPLES
    angle = product.astype(jnp.float32) * (2.0 * math.pi / SAMPLES)
    return jnp.concatenate([jnp.cos(angle), -jnp.sin(angle)], axis=0).astype(jnp.bfloat16)


def local(spectra, pair_bin, pair_valid, stack_in):
    white = whiten_band(spectra)
    band_width = spectra.shape[2]
    band_start = lax.axis_index("frq") * band_width
    pieces = []
    for turn in range(ROUNDS):
        partner = passed_along(white, "stn", turn + 1)
        pieces.append(cross_block(white, partner))
    cross_all = jnp.concatenate(pieces, axis=0)
    lag_parts = []
    for block in range(LAGS // LBLK):
        table = lag_table(band_start, band_width, block * LBLK, LBLK)
        lag_parts.append(jnp.dot(cross_all, table, preferred_element_type=jnp.float32))
    partial_corr = jnp.concatenate(lag_parts, axis=1)
    half_lags = stack_in.shape[1]
    valid = pair_valid.astype(jnp.float32)
    owners = lax.axis_size("stn")
    bins = pair_bin[:, 0]
    onehot = (bins[:, None] == lax.iota(jnp.int32, owners)[None, :]).astype(jnp.int32)
    onehot_float = onehot.astype(jnp.float32)
    total = lax.psum(partial_corr, "frq")
    mine = lax.dynamic_slice_in_dim(total, lax.axis_index("frq") * half_lags, half_lags, 1)
    weighted = mine * (1.0 / FREQ) * valid[:, None]
    bin_sums = jnp.dot(
        onehot_float.T,
        weighted,
        precision=lax.Precision.HIGHEST,
        preferred_element_type=jnp.float32,
    )
    owned = lax.psum_scatter(bin_sums, "stn", scatter_dimension=0, tiled=True)
    return stack_in + owned


def solution(mesh):
    placed = (P("stn", None, "frq"), P("stn", None), P("stn"), P("stn", "frq"))
    return jax.shard_map(
        local, mesh=mesh, in_specs=placed, out_specs=P("stn", "frq"), check_vma=False
    )
```

profile of v0, /device:TPU:1, one launch (start us, length us, event | category | flops | bytes accessed | tf_op | source)
XLA Modules:
  0.0 768.8 jit_solution(1959269469539100094)
XLA Ops:
  6.5 1.0 fusion.43
  7.5 0.2 reduce_sum.14
  7.7 0.2 reduce_sum.18
  7.9 0.2 div.21
  8.1 0.2 div.22
  8.4 1.0 fusion.53
  9.4 2.8 collective-permute-start
  12.1 1.5 collective-permute-start.1
  13.7 0.5 collective-permute-start.2
  14.1 1.6 collective-permute-start.3
  15.8 139.8 %cosine_convert_fusion.3 = (bf16[4096,512]{1,0:T(8,128)(2,1)}, bf16[4096,512]{1,0:T(8,128)(2,1)}, bf16[4096,512]{1,0:T(8,128)(2,1)S(1)}, bf16[4096,512]{1,0:T(8,...) fusion(s32[512]{0:T(512)S(1)} %iota_add_fusion.3, ...), kind=kLoop, calls=%fused_computation.55 | loop fusion | flops 142606336 | bytes 33576960 | tf_op jit(solution)/shard_map/convert.6
  155.6 0.0 collective-permute-done
  155.7 0.0 collective-permute-done.1
  155.8 0.0 collective-permute-done.3
  155.9 2.3 fusion.34
  158.1 7.3 fusion.12
  165.4 7.3 fusion.16
  172.8 6.1 fusion.20
  178.9 4.1 fusion.24
  183.1 0.0 copy-start.5
  183.1 0.0 copy-start.4
  183.1 0.0 copy-start.6
  183.1 0.0 copy-start.3
  183.1 1.5 pad_maximum_fusion
  184.6 0.0 all-reduce.4.cloned.1.call-update
  184.6 0.0 all-reduce.6.cloned.1.call-start
  184.7 72.5 %all-reduce.4.cloned.1.call-done = f32[256,2048]{1,0:T(8,128)} async-done(((f32[256,2048]{1,0:T(8,128)}), f32[256,2048]{1,0:T(8,128)}) %all-reduce.4.cloned.1.call-update) | async-done | bytes 2097168 | tf_op jit(solution)/shard_map/psum | solution.py:72
  257.3 2.8 fusion.31
  260.1 0.0 all-reduce.6.cloned.1.call-update
  260.1 0.6 dynamic-slice
  260.7 499.2 %all-reduce.6.cloned.1.call-done = f32[64,1024]{1,0:T(8,128)} async-done(((f32[64,1024]{1,0:T(8,128)}), f32[64,1024]{1,0:T(8,128)}) %all-reduce.6.cloned.1.call-update) | async-done | bytes 262160
  760.0 2.0 dynamic-slice_add_fusion
  (26 shorter events, 0.2 us)
Async XLA Ops:
  6.5 250.7 %all-reduce.4.cloned.1.call-start = ((), (), s32[]{:S(2)}) async-start(), calls=%async_computation | async-start | bytes 4194304 | tf_op jit(solution)/shard_map/psum | solution.py:72
  9.4 146.2 %collective-permute-start = (bf16[8,2,4096]{2,0,1:T(8,128)(2,1)S(1)}, bf16[8,2,4096]{2,0,1:T(8,128)(2,1)S(1)}, u32[]{:S(2)}, u32[]{:S(2)}) collective-permute-start(bf16[8,2,4096]{2,0,1:T(8,128)(2,1)S(1)} %get-tuple-element.6), channel_id=1, source_target_pairs={{0,2},{2,4},{4,6},{6,8},{8,10},{10,12},{12,14},{14,16},{16,18},{18... | collective-permute-start | bytes 393224 | tf_op jit(solution)/shard_map/ppermute | solution.py:19
  12.1 143.5 %collective-permute-start.1 = (bf16[8,2,4096]{2,0,1:T(8,128)(2,1)S(1)}, bf16[8,2,4096]{2,0,1:T(8,128)(2,1)S(1)}, u32[]{:S(2)}, u32[]{:S(2)}) collective-permute-start(bf16[8,2,4096]{2,0,1:T(8,128)(2,1)S(1)} %get-tuple-element.6), channel_id=1, source_target_pairs={{0,4},{2,6},{4,8},{6,10},{8,12},{10,14},{12,16},{14,18},{16,20},{1... | collective-permute-start | bytes 393224 | tf_op jit(solution)/shard_map/ppermute | solution.py:19
  13.7 142.1 %collective-permute-start.2 = (bf16[8,2,4096]{2,0,1:T(8,128)(2,1)S(1)}, bf16[8,2,4096]{2,0,1:T(8,128)(2,1)S(1)}, u32[]{:S(2)}, u32[]{:S(2)}) collective-permute-start(bf16[8,2,4096]{2,0,1:T(8,128)(2,1)S(1)} %get-tuple-element.6), channel_id=1, source_target_pairs={{0,6},{2,8},{4,10},{6,12},{8,14},{10,16},{12,18},{14,20},{16,22},{... | collective-permute-start | bytes 393224 | tf_op jit(solution)/shard_map/ppermute | solution.py:19
  14.1 141.7 %collective-permute-start.3 = (bf16[8,2,4096]{2,0,1:T(8,128)(2,1)S(1)}, bf16[8,2,4096]{2,0,1:T(8,128)(2,1)S(1)}, u32[]{:S(2)}, u32[]{:S(2)}) collective-permute-start(bf16[8,2,4096]{2,0,1:T(8,128)(2,1)S(1)} %get-tuple-element.6), channel_id=1, source_target_pairs={{0,8},{2,10},{4,12},{6,14},{8,16},{10,18},{12,20},{14,22},{16,24},... | collective-permute-start | bytes 393224 | tf_op jit(solution)/shard_map/ppermute | solution.py:19
  178.9 4.1 copy-start
  178.9 4.1 copy-start.1
  178.9 4.1 copy-start.2
  183.1 1.6 copy-start.5
  183.1 74.2 %copy-start.4 = (s32[256,1]{0,1:T(1,128)S(1)}, s32[256,1]{0,1:T(1,128)}, u32[]{:S(2)}) copy-start(s32[256,1]{0,1:T(1,128)} %param.5) | copy-start | bytes 3076
  183.1 77.0 %copy-start.6 = (u32[128]{0:T(128)S(1)}, u32[128]{0:T(128)}, u32[]{:S(2)}) copy-start(u32[128]{0:T(128)} %constant.64) | copy-start | bytes 1540
  183.1 576.9 %copy-start.3 = (f32[1,1024]{1,0:T(1,128)S(1)}, f32[1,1024]{1,0:T(1,128)}, u32[]{:S(2)}) copy-start(f32[1,1024]{1,0:T(1,128)} %param.7) | copy-start | bytes 12292
  184.6 575.3 %all-reduce.6.cloned.1.call-start = ((), (), s32[]{:S(2)}) async-start(), calls=%async_computation.1 | async-start | bytes 524288
Sparse Core Ops, SparseCore 0:
  184.8 72.4 all-reduce.3
  260.2 499.6 all-reduce.5
where the time goes:
time: 770 us; the launch traced here: 769 us
  waiting for transfers between devices  572 us (74%)
  other arithmetic  148 us (19%)
  matrix products  27.7 us (4%)
  between operations  13.6 us (2%)
    unnamed x3, waiting for transfers between devices  499 us
    another operation x1, other arithmetic  140 us
    psum x1, waiting for transfers between devices, local(): total = lax.psum(partial_corr, 'frq')  72.5 us
    dot_general x4, matrix products, local(): jnp.dot(cross_all, table, preferred_element_type=jnp.float32)  24.9 us
  transfers between devices with their start and end apart: 6, of which 2 were waited for; matrix products, arithmetic and copies ran while one was open for 18% of the time, Pallas kernels for 0%

commit v1 on v0

v1 whole, which is shorter than its diff:
```python
import functools
import math

import jax
import jax.numpy as jnp
import numpy as np
from jax import lax
from jax.experimental import pallas as pl
from jax.experimental.pallas import tpu as pltpu
from jax.sharding import PartitionSpec as P

ROUNDS = 4
FREQ = 8192
SAMPLES = 32768
LAGS = 2048
WBLK = 32
STN = 8
BINS = 64
N_STN = 64
N_FRQ = 2
BAND = FREQ // N_FRQ
CHUNK = BAND // N_STN
LANES = 2 * CHUNK
SOURCES = N_STN * N_FRQ
HALF = LAGS // N_FRQ
GROUP = 4
GROUPS = N_STN // GROUP
PERIOD = SAMPLES // CHUNK
PAIRS_DEV = ROUNDS * STN * STN
MESH = pl.DeviceIdType.MESH


def hops(offset):
    return (0, 1, 2, 1)[offset // 4] + (0, 1, 2, 1)[offset % 4]


FAR_FIRST = sorted(range(GROUPS), key=hops, reverse=True)


def tables():
    chunk = np.arange(SOURCES)[:, None] * np.arange(PERIOD)[None, :] % PERIOD
    angle = chunk * (2.0 * math.pi / PERIOD)
    coarse = np.concatenate([np.cos(angle), np.sin(angle)], axis=0).astype(np.float32)
    high = coarse.astype(jnp.bfloat16)
    low = (coarse - high.astype(np.float32)).astype(jnp.bfloat16)
    lag = np.arange(N_FRQ)[:, None, None] * HALF - LAGS // 2 + np.arange(HALF)[None, None, :]
    product = (np.arange(CHUNK)[None, :, None] + 1) * lag % SAMPLES
    turn = product * (2.0 * math.pi / SAMPLES)
    fine = np.concatenate([np.cos(turn), -np.sin(turn)], axis=1) / FREQ
    return high, low, fine.astype(np.float32)


def kernel(
    x_hbm, bin_ref, valid_ref, stack_ref, high_hbm, low_hbm, fine_hbm, out_ref,
    x, send, recv, key_send, keys, first, second, third, fourth, sums, gathered,
    high, low, fine, load_sem, table_sem, send_sem, key_send_sem, recv_sem, key_sem, row_send_sem, row_sem,
):
    me = lax.axis_index("stn")
    band = lax.axis_index("frq")
    my_group = me // GROUP
    my_x, my_z, my_w = me // 16, me // 4 % 4, me % 4

    def peer(offset, turn):
        x_at = (my_x + offset // 4) % 4
        z_at = (my_z + offset % 4) % 4
        return x_at * 16 + z_at * 4 + (my_w + turn) % 4

    load = pltpu.make_async_copy(x_hbm, x, load_sem)
    load.start()
    table_copies = [
        pltpu.make_async_copy(high_hbm, high, table_sem.at[0]),
        pltpu.make_async_copy(low_hbm, low, table_sem.at[1]),
        pltpu.make_async_copy(fine_hbm.at[band], fine, table_sem.at[2]),
    ]

    barrier = pltpu.get_barrier_semaphore()
    for offset in FAR_FIRST:

        def greet(turn, carry, offset=offset):
            pl.semaphore_signal(barrier, inc=1, device_id=(peer(offset, turn), band), device_id_type=MESH)
            return carry

        lax.fori_loop(0 if offset else 1, GROUP, greet, 0)
    pl.semaphore_signal(barrier, inc=1, device_id=(me, 1 - band), device_id_type=MESH)
    for copy in table_copies:
        copy.start()

    lane = lax.broadcasted_iota(jnp.int32, (STN, LANES), 1)
    is_real = lane < CHUNK
    same_block = (
        lax.broadcasted_iota(jnp.int32, (LANES, LANES), 0) // WBLK
        == lax.broadcasted_iota(jnp.int32, (LANES, LANES), 1) // WBLK
    )
    averaging = jnp.where(same_block, 1.0 / (2 * WBLK), 0.0).astype(jnp.bfloat16)

    load.wait()
    wide = 8

    def whiten(step, carry):
        values = []
        for part in range(wide):
            at = pl.multiple_of((step * wide + part) * LANES, LANES)
            both = x[:, :, pl.ds(at, LANES)].astype(jnp.float32)
            values.append((both[:, 0, :], both[:, 1, :]))
        squares = jnp.concatenate([re * re + im * im for re, im in values], axis=0)
        squares_high = squares.astype(jnp.bfloat16)
        squares_low = (squares - squares_high.astype(jnp.float32)).astype(jnp.bfloat16)
        power = jnp.dot(squares_high, averaging, preferred_element_type=jnp.float32) + jnp.dot(
            squares_low, averaging, preferred_element_type=jnp.float32
        )
        scale = lax.rsqrt(power + 1e-06)
        for part, (re, im) in enumerate(values):
            own = scale[part * STN : (part + 1) * STN]
            re, im = re * own, im * own
            even = jnp.where(is_real, re, pltpu.roll(im, CHUNK, 1))
            odd = jnp.where(is_real, pltpu.roll(re, CHUNK, 1), im)
            send[2 * (step * wide + part)] = even.astype(jnp.bfloat16)
            send[2 * (step * wide + part) + 1] = odd.astype(jnp.bfloat16)
        return carry

    lax.fori_loop(0, BAND // LANES // wide, whiten, 0)
    own_key = jnp.where(valid_ref[...] > 0, bin_ref[...], BINS)
    key_send[...] = own_key
    keys[me] = own_key
    recv[me] = send[me]

    pl.semaphore_wait(barrier, N_STN)

    for offset in FAR_FIRST:

        def post(turn, carry, offset=offset):
            to = peer(offset, turn)
            pltpu.make_async_remote_copy(
                src_ref=send.at[to],
                dst_ref=recv.at[me],
                send_sem=send_sem,
                recv_sem=recv_sem.at[my_group],
                device_id=(to, band),
                device_id_type=MESH,
            ).start()
            pltpu.make_async_remote_copy(
                src_ref=key_send,
                dst_ref=keys.at[me],
                send_sem=key_send_sem,
                recv_sem=key_sem.at[my_group],
                device_id=(to, band),
                device_id_type=MESH,
            ).start()
            return carry

        lax.fori_loop(0 if offset else 1, GROUP, post, 0)

    def await_group(group, count):
        some = recv.at[pl.ds(0, count)]
        pltpu.make_async_copy(some, some, recv_sem.at[group]).wait()
        some = keys.at[pl.ds(0, count)]
        pltpu.make_async_copy(some, some, key_sem.at[group]).wait()

    def unpack_group(group):
        for part in range(GROUP):
            block = group * GROUP + part
            white = recv[block].astype(jnp.float32)
            swapped = pltpu.roll(white, CHUNK, 1)
            first[block] = white
            second[block] = swapped
            third[block] = jnp.where(is_real, white, swapped)
            fourth[block] = jnp.where(is_real, swapped, -white)

    bin_row = lax.broadcasted_iota(jnp.int32, (BINS, LANES), 0)

    def bin_group(group):
        total = jnp.zeros((BINS, LANES), jnp.float32)
        for part in range(GROUP):
            block = group * GROUP + part
            partners = [(block + N_STN - turn - 1) % N_STN for turn in range(ROUNDS)]
            straight = [third[partner] for partner in partners]
            crossed = [fourth[partner] for partner in partners]
            pieces = []
            for turn in range(ROUNDS):
                for i in range(STN):
                    own = jnp.broadcast_to(first[block, pl.ds(i, 1), :], (STN, LANES))
                    other = jnp.broadcast_to(second[block, pl.ds(i, 1), :], (STN, LANES))
                    pieces.append(own * straight[turn] + other * crossed[turn])
            cross = jnp.concatenate(pieces, axis=0).astype(jnp.bfloat16)
            onehot = jnp.concatenate(
                [
                    jnp.where(keys[block, pl.ds(row, 1), :] == bin_row, 1.0, 0.0).astype(jnp.bfloat16)
                    for row in range(PAIRS_DEV // LANES)
                ],
                axis=1,
            )
            total += jnp.dot(onehot, cross, preferred_element_type=jnp.float32)
        return total

    await_group(my_group, GROUP - 1)
    unpack_group(my_group)

    def advance(step, total):
        early = step < 9
        side = (step + 1) // 2
        even = step % 2 == 0
        target = jnp.where(early, jnp.where(even, GROUPS - side, side), step - 4)
        needed = jnp.where(early, jnp.where(even, GROUPS - side - 1, side), step - 4)
        needed = (my_group + needed) % GROUPS
        await_group(needed, GROUP)
        unpack_group(needed)
        return total + bin_group((my_group + target) % GROUPS)

    total = lax.fori_loop(0, GROUPS - 1, advance, jnp.zeros((BINS, LANES), jnp.float32))
    total = total + bin_group((my_group + 11) % GROUPS)
    sums[...] = total.reshape(BINS, 1, LANES)
    slot = band * N_STN + me
    gathered[slot] = sums[me]

    for offset in FAR_FIRST:

        def deliver(turn, carry, offset=offset):
            to = peer(offset, turn)
            for there in (1 - band, band):
                pltpu.make_async_remote_copy(
                    src_ref=sums.at[to],
                    dst_ref=gathered.at[slot],
                    send_sem=row_send_sem,
                    recv_sem=row_sem,
                    device_id=(to, there),
                    device_id_type=MESH,
                ).start()
            return carry

        lax.fori_loop(0 if offset else 1, GROUP, deliver, 0)
    pltpu.make_async_remote_copy(
        src_ref=sums.at[me],
        dst_ref=gathered.at[slot],
        send_sem=row_send_sem,
        recv_sem=row_sem,
        device_id=(me, 1 - band),
        device_id_type=MESH,
    ).start()

    for copy in table_copies:
        copy.wait()
    some = send.at[pl.ds(0, N_STN - 1)]
    pltpu.make_async_copy(some, some, send_sem).wait()
    some = keys.at[pl.ds(0, N_STN - 1)]
    pltpu.make_async_copy(some, some, key_send_sem).wait()
    some = gathered.at[pl.ds(0, SOURCES - 1)]
    pltpu.make_async_copy(some, some, row_send_sem).wait()
    pltpu.make_async_copy(some, some, row_sem).wait()

    spectrum = gathered[...].reshape(SOURCES, LANES).T
    turned = jnp.concatenate([-spectrum[CHUNK:], spectrum[:CHUNK]], axis=0)
    left = jnp.concatenate([spectrum, turned], axis=1)
    left_high = left.astype(jnp.bfloat16)
    left_low = (left - left_high.astype(jnp.float32)).astype(jnp.bfloat16)
    mixed = (
        jnp.dot(left_high, high[...], preferred_element_type=jnp.float32)
        + jnp.dot(left_low, high[...], preferred_element_type=jnp.float32)
        + jnp.dot(left_high, low[...], preferred_element_type=jnp.float32)
    )
    for part in range(HALF // PERIOD):
        at = pl.ds(part * PERIOD, PERIOD)
        out_ref[:, at] = stack_ref[:, at] + jnp.sum(mixed * fine[:, at], axis=0, keepdims=True)


def local(spectra, pair_bin, pair_valid, stack_in):
    high, low, fine = tables()
    rows = PAIRS_DEV // LANES
    vmem = pl.BlockSpec(memory_space=pltpu.VMEM)
    anywhere = pl.BlockSpec(memory_space=pl.ANY)
    block = (N_STN, STN, LANES)
    return pl.pallas_call(
        kernel,
        out_shape=jax.ShapeDtypeStruct((1, HALF), jnp.float32),
        in_specs=[anywhere, vmem, vmem, vmem, anywhere, anywhere, anywhere],
        out_specs=vmem,
        scratch_shapes=[
            pltpu.VMEM((STN, 2, BAND), jnp.bfloat16),
            pltpu.VMEM(block, jnp.bfloat16),
            pltpu.VMEM(block, jnp.bfloat16),
            pltpu.VMEM((rows, LANES), jnp.int32),
            pltpu.VMEM((N_STN, rows, LANES), jnp.int32),
            pltpu.VMEM(block, jnp.float32),
            pltpu.VMEM(block, jnp.float32),
            pltpu.VMEM(block, jnp.float32),
            pltpu.VMEM(block, jnp.float32),
            pltpu.VMEM((BINS, 1, LANES), jnp.float32),
            pltpu.VMEM((SOURCES, 1, LANES), jnp.float32),
            pltpu.VMEM(high.shape, jnp.bfloat16),
            pltpu.VMEM(low.shape, jnp.bfloat16),
            pltpu.VMEM(fine.shape[1:], jnp.float32),
            pltpu.SemaphoreType.DMA,
            pltpu.SemaphoreType.DMA((3,)),
            pltpu.SemaphoreType.DMA,
            pltpu.SemaphoreType.DMA,
            pltpu.SemaphoreType.DMA((GROUPS,)),
            pltpu.SemaphoreType.DMA((GROUPS,)),
            pltpu.SemaphoreType.DMA,
            pltpu.SemaphoreType.DMA,
        ],
        compiler_params=pltpu.CompilerParams(
            collective_id=0, has_side_effects=True, vmem_limit_bytes=32 * 2**20
        ),
    )(
        spectra,
        pair_bin.reshape(rows, LANES),
        pair_valid.reshape(rows, LANES),
        stack_in,
        jnp.asarray(high),
        jnp.asarray(low),
        jnp.asarray(fine),
    )


def solution(mesh):
    placed = (P("stn", None, "frq"), P("stn", None), P("stn"), P("stn", "frq"))
    return jax.shard_map(
        local, mesh=mesh, in_specs=placed, out_specs=P("stn", "frq"), check_vma=False
    )
```

time: 770 us -> 33.1 us (0.04)
  waiting for transfers between devices: 572 us -> 0 us
  other arithmetic: 148 us -> 0 us
  matrix products: 27.7 us -> 0 us
  Pallas kernels: 0 us -> 26.8 us
  between operations: 13.6 us -> 0.02 us
    unnamed x3 -> x0, waiting for transfers between devices: 499 us -> none
    another operation x1 -> x0, other arithmetic: 140 us -> none
    psum x1 -> x0, waiting for transfers between devices: 72.5 us -> none  [local(): total = lax.psum(partial_corr, 'frq')]
    dot_general x5 -> x0, matrix products: 27.7 us -> none  [the longest x4 24.9 us: local(): jnp.dot(cross_all, table, preferred_element_type=jnp.float32)]
    pallas_call x0 -> x1, Pallas kernels: none -> 26.8 us  [local(): pl.pallas_call(kernel, out_shape=jax.ShapeDtypeStruct((1, HALF), jnp.floa...]
  transfers between devices with their start and end apart: 6 -> 0, of which waited for: 2 -> 0; matrix products, arithmetic and copies ran while one was open for 18% -> 0% of each run, Pallas kernels for 0% -> 0%
where the time goes in v1:
time: 33.1 us; the launch traced here: 32.8 us
  Pallas kernels  26.8 us (81%)
  local copies, waits for them, and re-layouts  6 us (18%)
    pallas_call x1, Pallas kernels, local(): pl.pallas_call(kernel, out_shape=jax.ShapeDtypeStruct((1, HALF), jnp.floa...  26.8 us
    unnamed x15, local copies, waits for them, and re-layouts  6 us

profile of v1, /device:TPU:1, one launch (start us, length us, event | category | flops | bytes accessed | tf_op | source)
XLA Modules:
  0.0 32.8 jit_solution(3399674702472304061)
XLA Ops:
  0.0 0.0 copy-start.6
  0.0 0.0 copy-start.5
  0.0 0.7 %copy-done.6 = s32[256]{0:T(256)S(1)} copy-done((s32[256]{0:T(256)S(1)}, s32[256]{0:T(256)}, u32[]{:S(2)}) %copy-start.6) | copy-done | bytes 1048
  0.7 0.0 copy-done.5
  0.7 0.0 copy-start
  0.7 1.2 %copy-done = f32[2,128,1024]{2,1,0:T(8,128)S(1)} copy-done((f32[2,128,1024]{2,1,0:T(8,128)S(1)}, f32[2,128,1024]{2,1,0:T(8,128)}, u32[]{:S(2)}) %copy-start) | copy-done | bytes 1048600
  1.9 0.0 copy-start.1
  1.9 0.9 %copy-done.1 = bf16[256,512]{1,0:T(8,128)(2,1)S(1)} copy-done((bf16[256,512]{1,0:T(8,128)(2,1)S(1)}, bf16[256,512]{1,0:T(8,128)(2,1)}, u32[]{:S(2)}) %copy-start.1) | copy-done | bytes 262168
  2.9 0.0 copy-start.2
  2.9 0.9 %copy-done.2 = bf16[256,512]{1,0:T(8,128)(2,1)S(1)} copy-done((bf16[256,512]{1,0:T(8,128)(2,1)S(1)}, bf16[256,512]{1,0:T(8,128)(2,1)}, u32[]{:S(2)}) %copy-start.2) | copy-done | bytes 262168
  3.8 0.0 copy-start.3
  3.8 0.9 %copy-done.3 = bf16[8,2,4096]{2,1,0:T(2,128)(2,1)S(1)} copy-done((bf16[8,2,4096]{2,1,0:T(2,128)(2,1)S(1)}, bf16[8,2,4096]{2,1,0:T(2,128)(2,1)}, u32[]{:S(2)}) %copy-start.3) | copy-done | bytes 131096
  4.7 0.0 copy-start.4
  4.7 0.7 %copy-done.4 = f32[1,1024]{1,0:T(1,128)S(1)} copy-done((f32[1,1024]{1,0:T(1,128)S(1)}, f32[1,1024]{1,0:T(1,128)}, u32[]{:S(2)}) %copy-start.4) | copy-done | bytes 4120
  5.4 26.8 %shard_map.73 = f32[1,1024]{1,0:T(1,128)S(1)} custom-call(bf16[8,2,4096]{2,1,0:T(2,128)(2,1)S(1)} %copy-done.3, s32[2,128]{1,0:T(2,128)S(1)} %bitcast.2, s32[2,128]{1,0:T(2,128)S(1)} %bitcast.3, f32[1,1024]{1,0:T(1,128)S(1)} %copy-done.4, bf16[256,512]{1,0:T(8,128)(2,1)S(1)} %copy-done.2, bf16[256,512]{1,0:T(8,128)(2,1)S(1)} %copy-done.1, ...), custom_call_target="tpu_custom_call" | custom-call | tf_op jit(solution)/shard_map/pallas_call | solution.py:271
  32.2 0.6 %copy.9 = f32[1,1024]{1,0:T(1,128)} copy(f32[1,1024]{1,0:T(1,128)S(1)} %shard_map.73) | data formatting | bytes 8192
Async XLA Ops:
  0.0 0.7 %copy-start.6 = (s32[256]{0:T(256)S(1)}, s32[256]{0:T(256)}, u32[]{:S(2)}) copy-start(s32[256]{0:T(256)} %param.9) | copy-start | bytes 3076
  0.0 0.7 %copy-start.5 = (s32[256,1]{0,1:T(1,128)S(1)}, s32[256,1]{0,1:T(1,128)}, u32[]{:S(2)}) copy-start(s32[256,1]{0,1:T(1,128)} %param.8) | copy-start | bytes 3076
  0.7 1.2 %copy-start = (f32[2,128,1024]{2,1,0:T(8,128)S(1)}, f32[2,128,1024]{2,1,0:T(8,128)}, u32[]{:S(2)}) copy-start(f32[2,128,1024]{2,1,0:T(8,128)} %constant.8.clone.fine_hbm) | copy-start | bytes 3145732
  1.9 0.9 %copy-start.1 = (bf16[256,512]{1,0:T(8,128)(2,1)S(1)}, bf16[256,512]{1,0:T(8,128)(2,1)}, u32[]{:S(2)}) copy-start(bf16[256,512]{1,0:T(8,128)(2,1)} %constant.7.clone.low_hbm) | copy-start | bytes 786436
  2.9 0.9 %copy-start.2 = (bf16[256,512]{1,0:T(8,128)(2,1)S(1)}, bf16[256,512]{1,0:T(8,128)(2,1)}, u32[]{:S(2)}) copy-start(bf16[256,512]{1,0:T(8,128)(2,1)} %constant.6.clone.high_hbm) | copy-start | bytes 786436
  3.8 0.9 %copy-start.3 = (bf16[8,2,4096]{2,1,0:T(2,128)(2,1)S(1)}, bf16[8,2,4096]{2,1,0:T(2,128)(2,1)}, u32[]{:S(2)}) copy-start(bf16[8,2,4096]{2,1,0:T(2,128)(2,1)} %x_hbm.1) | copy-start | bytes 393220
  4.7 0.7 %copy-start.4 = (f32[1,1024]{1,0:T(1,128)S(1)}, f32[1,1024]{1,0:T(1,128)}, u32[]{:S(2)}) copy-start(f32[1,1024]{1,0:T(1,128)} %stack_ref.1) | copy-start | bytes 12292

commit v2 on v1

v2 whole, which is shorter than its diff:
```python
import functools
import math

import jax
import jax.numpy as jnp
import numpy as np
from jax import lax
from jax.experimental import pallas as pl
from jax.experimental.pallas import tpu as pltpu
from jax.sharding import PartitionSpec as P

ROUNDS = 4
FREQ = 8192
SAMPLES = 32768
LAGS = 2048
WBLK = 32
STN = 8
BINS = 64
N_STN = 64
N_FRQ = 2
BAND = FREQ // N_FRQ
CHUNK = BAND // N_STN
LANES = 2 * CHUNK
SOURCES = N_STN * N_FRQ
HALF = LAGS // N_FRQ
GROUP = 4
GROUPS = N_STN // GROUP
PERIOD = SAMPLES // CHUNK
PAIRS_DEV = ROUNDS * STN * STN
MESH = pl.DeviceIdType.MESH


def hops(offset):
    return (0, 1, 2, 1)[offset // 4] + (0, 1, 2, 1)[offset % 4]


FAR_FIRST = sorted(range(GROUPS), key=hops, reverse=True)


def tables():
    chunk = np.arange(SOURCES)[:, None] * np.arange(PERIOD)[None, :] % PERIOD
    angle = chunk * (2.0 * math.pi / PERIOD)
    coarse = np.concatenate([np.cos(angle), np.sin(angle)], axis=0).astype(np.float32)
    high = coarse.astype(jnp.bfloat16)
    low = (coarse - high.astype(np.float32)).astype(jnp.bfloat16)
    lag = np.arange(N_FRQ)[:, None, None] * HALF - LAGS // 2 + np.arange(HALF)[None, None, :]
    product = (np.arange(CHUNK)[None, :, None] + 1) * lag % SAMPLES
    turn = product * (2.0 * math.pi / SAMPLES)
    fine = np.concatenate([np.cos(turn), -np.sin(turn)], axis=1) / FREQ
    return high, low, fine.astype(np.float32)


def whiten_own(x, send, accs):
    is_real = lax.broadcasted_iota(jnp.int32, (STN, LANES), 1) < CHUNK
    square = (2 * LANES, 2 * LANES)
    same_block = (
        lax.broadcasted_iota(jnp.int32, square, 0) // WBLK
        == lax.broadcasted_iota(jnp.int32, square, 1) // WBLK
    )
    averaging = jnp.where(same_block, 1.0 / (2 * WBLK), 0.0).astype(jnp.bfloat16)
    for unit in range(len(accs)):
        pltpu.matmul_push_rhs(averaging, 0, unit)
    wide = 8

    def whiten(step, load):
        every = []
        for unit, acc in enumerate(accs):
            values = []
            for part in range(wide):
                at = pl.multiple_of(((step * len(accs) + unit) * wide + part) * LANES, LANES)
                both = x[:, :, pl.ds(at, LANES)].astype(jnp.float32)
                values.append((both[:, 0, :], both[:, 1, :]))
            every.append(values)
            squares = [re * re + im * im for re, im in values]
            squares = jnp.concatenate(
                [jnp.concatenate(squares[: wide // 2], axis=0), jnp.concatenate(squares[wide // 2 :], axis=0)],
                axis=1,
            )
            high = squares.astype(jnp.bfloat16)
            low = (squares - high.astype(jnp.float32)).astype(jnp.bfloat16)
            pltpu.matmul_acc_lhs(acc, high, load)
            pltpu.matmul_acc_lhs(acc, low)
        for unit, acc in enumerate(accs):
            scale = lax.rsqrt(pltpu.matmul_pop(acc) + 1e-06)
            for part, (re, im) in enumerate(every[unit]):
                row, column = part % (wide // 2) * STN, part // (wide // 2) * LANES
                own = scale[row : row + STN, column : column + LANES]
                re, im = re * own, im * own
                even = jnp.where(is_real, re, pltpu.roll(im, CHUNK, 1))
                odd = jnp.where(is_real, pltpu.roll(re, CHUNK, 1), im)
                chunk = 2 * ((step * len(accs) + unit) * wide + part)
                send[chunk] = even.astype(jnp.bfloat16)
                send[chunk + 1] = odd.astype(jnp.bfloat16)

    whiten(0, 0)

    def again(step, carry):
        whiten(step, None)
        return carry

    lax.fori_loop(1, BAND // LANES // wide // len(accs), again, 0)


def binning(recv, keys, first, second, third, fourth, halves):
    is_real = lax.broadcasted_iota(jnp.int32, (STN, LANES), 1) < CHUNK
    bin_row = lax.broadcasted_iota(jnp.int32, (BINS, LANES), 0)

    def twice(one, other):
        return jnp.concatenate([one, other], axis=0).astype(jnp.bfloat16)

    def unpack_group(group):
        for part in range(GROUP):
            block = group * GROUP + part
            white = recv[block].astype(jnp.float32)
            swapped = pltpu.roll(white, CHUNK, 1)
            straight = jnp.where(is_real, white, swapped)
            crossed = jnp.where(is_real, swapped, -white)
            first[block] = white
            second[block] = swapped
            third[block] = twice(straight, straight)
            fourth[block] = twice(crossed, crossed)

    def spread(ref, block, i):
        return twice(
            *(jnp.broadcast_to(ref[block, pl.ds(row, 1), :], (STN, LANES)) for row in (i, i + 1))
        )

    def cross_of(block):
        own = [(spread(first, block, i), spread(second, block, i)) for i in range(0, STN, 2)]
        pieces = []
        for turn in range(ROUNDS):
            partner = (block + N_STN - turn - 1) % N_STN
            straight, crossed = third[partner], fourth[partner]
            pieces += [one * straight + other * crossed for one, other in own]
        return jnp.concatenate(pieces, axis=0)

    def onehot_of(block):
        return jnp.concatenate(
            [
                jnp.where(keys[block, pl.ds(row, 1), :] == bin_row, 1.0, 0.0).astype(jnp.bfloat16)
                for row in range(PAIRS_DEV // LANES)
            ],
            axis=1,
        )

    def bin_group(group):
        for unit, half in enumerate(halves):
            blocks = [group * GROUP + 2 * unit + part for part in range(2)]
            pltpu.matmul_push_rhs(jnp.concatenate([cross_of(block) for block in blocks], axis=1), 0, unit)
            pltpu.matmul_acc_lhs(half, jnp.concatenate([onehot_of(block) for block in blocks], axis=0), 0)

    def binned():
        total = jnp.zeros((BINS, LANES), jnp.float32)
        for half in halves:
            product = pltpu.matmul_pop(half)
            total += product[:BINS, :LANES] + product[BINS:, LANES:]
        return total

    return unpack_group, bin_group, binned


def push_tables(high, low, accs):
    for unit in range(len(accs)):
        at = pl.ds(unit * 2 * LANES, 2 * LANES)
        pltpu.matmul_push_rhs(high[:, at], 0, unit)
        pltpu.matmul_push_rhs(low[:, at], 1, unit)


def transform(gathered, fine, stack_ref, out_ref, accs):
    spectrum = gathered[...].reshape(SOURCES, LANES).T
    turned = jnp.concatenate([-spectrum[CHUNK:], spectrum[:CHUNK]], axis=0)
    left = jnp.concatenate([spectrum, turned], axis=1)
    left_high = left.astype(jnp.bfloat16)
    left_low = (left - left_high.astype(jnp.float32)).astype(jnp.bfloat16)
    for acc in accs:
        pltpu.matmul_acc_lhs(acc, left_high, 0)
        pltpu.matmul_acc_lhs(acc, left_low)
        pltpu.matmul_acc_lhs(acc, left_high, 1)
    for unit, acc in enumerate(accs):
        mixed = pltpu.matmul_pop(acc)
        for part in range(HALF // PERIOD):
            at = pl.ds(part * PERIOD + unit * 2 * LANES, 2 * LANES)
            out_ref[:, at] = stack_ref[:, at] + jnp.sum(mixed * fine[:, at], axis=0, keepdims=True)


def kernel(
    x_hbm, bin_hbm, valid_hbm, stack_hbm, high_hbm, low_hbm, fine_hbm, out_ref,
    x, bin_ref, valid_ref, stack_ref, send, recv, key_send, keys, first, second, third, fourth, sums, gathered,
    high, low, fine, load_sem, table_sem, send_sem, key_send_sem, recv_sem, key_sem, row_send_sem, row_sem,
):
    me = lax.axis_index("stn")
    band = lax.axis_index("frq")
    my_group = me // GROUP
    my_x, my_z, my_w = me // 16, me // 4 % 4, me % 4

    def peer(offset, turn):
        x_at = (my_x + offset // 4) % 4
        z_at = (my_z + offset % 4) % 4
        return x_at * 16 + z_at * 4 + (my_w + turn) % 4

    load = pltpu.make_async_copy(x_hbm, x, load_sem)
    load.start()
    table_copies = [
        pltpu.make_async_copy(high_hbm, high, table_sem.at[0]),
        pltpu.make_async_copy(low_hbm, low, table_sem.at[1]),
        pltpu.make_async_copy(fine_hbm.at[band], fine, table_sem.at[2]),
        pltpu.make_async_copy(stack_hbm, stack_ref, table_sem.at[3]),
    ]
    bin_load = pltpu.make_async_copy(bin_hbm, bin_ref, table_sem.at[4])
    bin_load.start()
    valid_load = pltpu.make_async_copy(valid_hbm, valid_ref, table_sem.at[5])
    valid_load.start()

    barrier = pltpu.get_barrier_semaphore()
    for offset in FAR_FIRST:

        def greet(turn, carry, offset=offset):
            pl.semaphore_signal(barrier, inc=1, device_id=(peer(offset, turn), band), device_id_type=MESH)
            return carry

        lax.fori_loop(0 if offset else 1, GROUP, greet, 0)
    pl.semaphore_signal(barrier, inc=1, device_id=(me, 1 - band), device_id_type=MESH)
    for copy in table_copies:
        copy.start()

    load.wait()
    units = pltpu.ACC(0), pltpu.ACC(1)
    pl.run_scoped(
        lambda *accs: whiten_own(x, send, accs), *(unit((4 * STN, 2 * LANES), jnp.float32) for unit in units)
    )
    bin_load.wait()
    valid_load.wait()
    own_key = jnp.where(valid_ref[...] > 0, bin_ref[...], BINS)
    key_send[...] = own_key
    keys[me] = own_key
    recv[me] = send[me]

    pl.semaphore_wait(barrier, N_STN)

    for offset in FAR_FIRST:

        def post(turn, carry, offset=offset):
            to = peer(offset, turn)
            pltpu.make_async_remote_copy(
                src_ref=send.at[to],
                dst_ref=recv.at[me],
                send_sem=send_sem,
                recv_sem=recv_sem.at[my_group],
                device_id=(to, band),
                device_id_type=MESH,
            ).start()
            pltpu.make_async_remote_copy(
                src_ref=key_send,
                dst_ref=keys.at[me],
                send_sem=key_send_sem,
                recv_sem=key_sem.at[my_group],
                device_id=(to, band),
                device_id_type=MESH,
            ).start()
            return carry

        lax.fori_loop(0 if offset else 1, GROUP, post, 0)

    def await_group(group, count):
        some = recv.at[pl.ds(0, count)]
        pltpu.make_async_copy(some, some, recv_sem.at[group]).wait()
        some = keys.at[pl.ds(0, count)]
        pltpu.make_async_copy(some, some, key_sem.at[group]).wait()

    def plan(step):
        early = step < 9
        side = (step + 1) // 2
        even = step % 2 == 0
        target = jnp.where(early, jnp.where(even, GROUPS - side, side), step - 4)
        needed = jnp.where(early, jnp.where(even, GROUPS - side - 1, side), step - 4)
        return (my_group + target) % GROUPS, (my_group + needed) % GROUPS

    def correlate(*halves):
        unpack_group, bin_group, binned = binning(recv, keys, first, second, third, fourth, halves)
        await_group(my_group, GROUP - 1)
        unpack_group(my_group)
        needed = plan(0)[1]
        await_group(needed, GROUP)
        unpack_group(needed)

        def advance(step, carry):
            target, needed = plan(step - 1)[0], plan(step)[1]
            await_group(needed, GROUP)
            bin_group(target)
            unpack_group(needed)
            return carry

        lax.fori_loop(1, GROUPS - 1, advance, 0)
        bin_group(plan(GROUPS - 2)[0])
        bin_group(plan(GROUPS - 1)[0])
        sums[...] = binned().reshape(BINS, 1, LANES)

    pl.run_scoped(correlate, *(unit((2 * BINS, 2 * LANES), jnp.float32) for unit in units))
    slot = band * N_STN + me
    gathered[slot] = sums[me]

    for offset in FAR_FIRST:

        def deliver(turn, carry, offset=offset):
            to = peer(offset, turn)
            for there in (1 - band, band):
                pltpu.make_async_remote_copy(
                    src_ref=sums.at[to],
                    dst_ref=gathered.at[slot],
                    send_sem=row_send_sem,
                    recv_sem=row_sem,
                    device_id=(to, there),
                    device_id_type=MESH,
                ).start()
            return carry

        lax.fori_loop(0 if offset else 1, GROUP, deliver, 0)
    pltpu.make_async_remote_copy(
        src_ref=sums.at[me],
        dst_ref=gathered.at[slot],
        send_sem=row_send_sem,
        recv_sem=row_sem,
        device_id=(me, 1 - band),
        device_id_type=MESH,
    ).start()

    for copy in table_copies:
        copy.wait()

    def finish(*accs):
        push_tables(high, low, accs)
        some = gathered.at[pl.ds(0, SOURCES - 1)]
        pltpu.make_async_copy(some, some, row_sem).wait()
        transform(gathered, fine, stack_ref, out_ref, accs)

    pl.run_scoped(finish, *(unit((LANES, 2 * LANES), jnp.float32) for unit in units))
    some = send.at[pl.ds(0, N_STN - 1)]
    pltpu.make_async_copy(some, some, send_sem).wait()
    some = keys.at[pl.ds(0, N_STN - 1)]
    pltpu.make_async_copy(some, some, key_send_sem).wait()
    some = gathered.at[pl.ds(0, SOURCES - 1)]
    pltpu.make_async_copy(some, some, row_send_sem).wait()


def local(spectra, pair_bin, pair_valid, stack_in):
    high, low, fine = tables()
    rows = PAIRS_DEV // LANES
    vmem = pl.BlockSpec(memory_space=pltpu.VMEM)
    anywhere = pl.BlockSpec(memory_space=pltpu.HBM)
    block = (N_STN, STN, LANES)
    return pl.pallas_call(
        kernel,
        out_shape=jax.ShapeDtypeStruct((1, HALF), jnp.float32),
        in_specs=[anywhere] * 7,
        out_specs=vmem,
        scratch_shapes=[
            pltpu.VMEM((STN, 2, BAND), jnp.bfloat16),
            pltpu.VMEM((rows, LANES), jnp.int32),
            pltpu.VMEM((rows, LANES), jnp.int32),
            pltpu.VMEM((1, HALF), jnp.float32),
            pltpu.VMEM(block, jnp.bfloat16),
            pltpu.VMEM(block, jnp.bfloat16),
            pltpu.VMEM((rows, LANES), jnp.int32),
            pltpu.VMEM((N_STN, rows, LANES), jnp.int32),
            pltpu.VMEM(block, jnp.float32),
            pltpu.VMEM(block, jnp.float32),
            pltpu.VMEM((N_STN, 2 * STN, LANES), jnp.bfloat16),
            pltpu.VMEM((N_STN, 2 * STN, LANES), jnp.bfloat16),
            pltpu.VMEM((BINS, 1, LANES), jnp.float32),
            pltpu.VMEM((SOURCES, 1, LANES), jnp.float32),
            pltpu.VMEM(high.shape, jnp.bfloat16),
            pltpu.VMEM(low.shape, jnp.bfloat16),
            pltpu.VMEM(fine.shape[1:], jnp.float32),
            pltpu.SemaphoreType.DMA,
            pltpu.SemaphoreType.DMA((6,)),
            pltpu.SemaphoreType.DMA,
            pltpu.SemaphoreType.DMA,
            pltpu.SemaphoreType.DMA((GROUPS,)),
            pltpu.SemaphoreType.DMA((GROUPS,)),
            pltpu.SemaphoreType.DMA,
            pltpu.SemaphoreType.DMA,
        ],
        compiler_params=pltpu.CompilerParams(
            collective_id=0, has_side_effects=True, vmem_limit_bytes=32 * 2**20
        ),
    )(
        *(
            pltpu.with_memory_space_constraint(operand, pltpu.HBM)
            for operand in (
                spectra,
                pair_bin.reshape(rows, LANES),
                pair_valid.reshape(rows, LANES),
                stack_in,
                jnp.asarray(high),
                jnp.asarray(low),
                jnp.asarray(fine),
            )
        )
    )


def solution(mesh):
    placed = (P("stn", None, "frq"), P("stn", None), P("stn"), P("stn", "frq"))
    return jax.shard_map(
        local, mesh=mesh, in_specs=placed, out_specs=P("stn", "frq"), check_vma=False
    )
```

time: 33.1 us -> 24.6 us (0.74)
  local copies, waits for them, and re-layouts: 6 us -> 0.6 us
  Pallas kernels: 26.8 us -> 23.9 us
    unnamed x15 -> x1, local copies, waits for them, and re-layouts: 6 us -> 0.6 us
    pallas_call x1, Pallas kernels: 26.8 us -> 23.9 us  [local(): pl.pallas_call(kernel, out_shape=jax.ShapeDtypeStruct((1, HALF), jnp.floa...]
where the time goes in v2:
time: 24.6 us; the launch traced here: 24.5 us
  Pallas kernels  23.9 us (97%)
  local copies, waits for them, and re-layouts  0.6 us (2%)
    pallas_call x1, Pallas kernels, local(): pl.pallas_call(kernel, out_shape=jax.ShapeDtypeStruct((1, HALF), jnp.floa...  23.9 us
    unnamed x1, local copies, waits for them, and re-layouts  0.6 us

profile of v2, /device:TPU:1, one launch (start us, length us, event | category | flops | bytes accessed | tf_op | source)
XLA Modules:
  0.0 24.5 jit_solution(5355398729823955685)
XLA Ops:
  0.0 23.9 %shard_map.73 = f32[1,1024]{1,0:T(1,128)S(1)} custom-call(bf16[8,2,4096]{2,1,0:T(2,128)(2,1)} %x_hbm.1, s32[2,128]{1,0:T(2,128)} %bitcast.2, s32[2,128]{1,0:T(2,128)} %bitcast.3, f32[1,1024]{1,0:T(1,128)} %stack_hbm.1, bf16[256,512]{1,0:T(8,128)(2,1)} %constant.6.clone.high_hbm, bf16[256,512]{1,0:T(8,128)(2,1)} %constant.7.clone.low_hbm, ...), custom_call_target="tpu_custom_call" | custom-call | tf_op jit(solution)/shard_map/pallas_call | solution.py:351
  23.9 0.6 %copy.9 = f32[1,1024]{1,0:T(1,128)} copy(f32[1,1024]{1,0:T(1,128)S(1)} %shard_map.73) | data formatting | bytes 8192

commit v3 on v2

v3 whole, which is shorter than its diff:
```python
import functools
import math

import jax
import jax.numpy as jnp
import numpy as np
from jax import lax
from jax.experimental import pallas as pl
from jax.experimental.pallas import tpu as pltpu
from jax.sharding import PartitionSpec as P

ROUNDS = 4
FREQ = 8192
SAMPLES = 32768
LAGS = 2048
WBLK = 32
STN = 8
BINS = 64
N_STN = 64
N_FRQ = 2
BAND = FREQ // N_FRQ
LANES = 128
CHUNKS = BAND // LANES
SLOTS = N_FRQ * CHUNKS
HALF = LAGS // N_FRQ
GROUP = 4
GROUPS = N_STN // GROUP
PERIOD = SAMPLES // LANES
PAIRS_DEV = ROUNDS * STN * STN
ROWS = PAIRS_DEV // LANES
FAR_FIRST = (2, 1, 3, 0)
MESH = pl.DeviceIdType.MESH


def tables():
    chunk = np.arange(SLOTS)[:, None] * np.arange(PERIOD)[None, :] % PERIOD
    angle = chunk * (2.0 * math.pi / PERIOD)
    coarse = np.concatenate([np.cos(angle), np.sin(angle)], axis=0).astype(np.float32)
    coarse = np.concatenate([coarse, coarse], axis=0)
    high = coarse.astype(jnp.bfloat16)
    low = (coarse - high.astype(np.float32)).astype(jnp.bfloat16)
    lag = np.arange(N_FRQ)[:, None, None] * HALF - LAGS // 2 + np.arange(HALF)[None, None, :]
    product = (np.arange(LANES)[None, :, None] + 1) * lag % SAMPLES
    turn = product * (2.0 * math.pi / SAMPLES)
    fine = np.concatenate([np.cos(turn), -np.sin(turn)], axis=1) / FREQ
    return high, low, fine.astype(np.float32)


def twice(one, other):
    return jnp.concatenate([one, other], axis=0).astype(jnp.bfloat16)


def whiten_own(x, send, accs):
    square = (2 * LANES, 2 * LANES)
    same_block = (
        lax.broadcasted_iota(jnp.int32, square, 0) // WBLK
        == lax.broadcasted_iota(jnp.int32, square, 1) // WBLK
    )
    averaging = jnp.where(same_block, 1.0 / (2 * WBLK), 0.0).astype(jnp.bfloat16)
    for unit in range(len(accs)):
        pltpu.matmul_push_rhs(averaging, 0, unit)
    wide = 8

    def whiten(step, load):
        every = []
        for unit, acc in enumerate(accs):
            values = []
            for part in range(wide):
                at = pl.multiple_of(((step * len(accs) + unit) * wide + part) * LANES, LANES)
                both = x[:, :, pl.ds(at, LANES)].astype(jnp.float32)
                values.append((both[:, 0, :], both[:, 1, :]))
            every.append(values)
            squares = [re * re + im * im for re, im in values]
            squares = jnp.concatenate(
                [jnp.concatenate(squares[: wide // 2], axis=0), jnp.concatenate(squares[wide // 2 :], axis=0)],
                axis=1,
            )
            high = squares.astype(jnp.bfloat16)
            low = (squares - high.astype(jnp.float32)).astype(jnp.bfloat16)
            pltpu.matmul_acc_lhs(acc, high, load)
            pltpu.matmul_acc_lhs(acc, low)
        for unit, acc in enumerate(accs):
            scale = lax.rsqrt(pltpu.matmul_pop(acc) + 1e-06)
            for part, (re, im) in enumerate(every[unit]):
                row, column = part % (wide // 2) * STN, part // (wide // 2) * LANES
                own = scale[row : row + STN, column : column + LANES]
                send[(step * len(accs) + unit) * wide + part] = twice(re * own, im * own)

    whiten(0, 0)

    def again(step, carry):
        whiten(step, None)
        return carry

    lax.fori_loop(1, CHUNKS // wide // len(accs), again, 0)


def binning(recv, keys, real, imag, reals, imags, halves):
    bin_row = lax.broadcasted_iota(jnp.int32, (BINS, LANES), 0)

    def unpack_group(group):
        for part in range(GROUP):
            block = group * GROUP + part
            white = recv[block].astype(jnp.float32)
            re, im = white[:STN], white[STN:]
            real[block] = re
            imag[block] = im
            reals[block] = twice(re, re)
            imags[block] = twice(im, im)

    def spread(ref, block, i):
        return twice(
            *(jnp.broadcast_to(ref[block, pl.ds(row, 1), :], (STN, LANES)) for row in (i, i + 1))
        )

    def cross_of(block):
        own = [(spread(real, block, i), spread(imag, block, i)) for i in range(0, STN, 2)]
        real_part, imag_part = [], []
        for turn in range(ROUNDS):
            partner = (block + N_STN - turn - 1) % N_STN
            re, im = reals[partner], imags[partner]
            real_part += [one * re + other * im for one, other in own]
            imag_part += [other * re - one * im for one, other in own]
        return jnp.concatenate(
            [jnp.concatenate(real_part, axis=0), jnp.concatenate(imag_part, axis=0)], axis=1
        )

    def onehot_of(block):
        return jnp.concatenate(
            [
                jnp.where(keys[block, pl.ds(row, 1), :] == bin_row, 1.0, 0.0).astype(jnp.bfloat16)
                for row in range(ROWS)
            ],
            axis=1,
        )

    def bin_group(group):
        for part in range(GROUP):
            block = group * GROUP + part
            unit, stage = part % 2, part // 2
            pltpu.matmul_push_rhs(cross_of(block), stage, unit)
            pltpu.matmul_acc_lhs(halves[unit], onehot_of(block), stage)

    def binned():
        return pltpu.matmul_pop(halves[0]) + pltpu.matmul_pop(halves[1])

    return unpack_group, bin_group, binned


def push_tables(high, low, accs):
    for unit in range(len(accs)):
        pltpu.matmul_push_rhs(high[...], 0, unit)
        pltpu.matmul_push_rhs(low[...], 1, unit)


def transform(gathered, fine, stack_ref, out_ref, accs):
    spectrum = gathered[...].reshape(SLOTS, 2 * LANES)
    re, im = spectrum[:, :LANES], spectrum[:, LANES:]
    for acc, upper, lower in zip(accs, (re, im), (-im, re)):
        left = jnp.concatenate([upper, lower], axis=0).T
        left_high = left.astype(jnp.bfloat16)
        left_low = (left - left_high.astype(jnp.float32)).astype(jnp.bfloat16)
        left = jnp.concatenate([left_high, left_low], axis=1)
        pltpu.matmul_acc_lhs(acc, left, 0)
        pltpu.matmul_acc_lhs(acc, left, 1)
    mixed = [pltpu.matmul_pop(acc) for acc in accs]
    for part in range(HALF // PERIOD):
        at = pl.ds(part * PERIOD, PERIOD)
        total = sum(
            jnp.sum(one * fine[pl.ds(unit * LANES, LANES), at], axis=0, keepdims=True)
            for unit, one in enumerate(mixed)
        )
        out_ref[:, at] = stack_ref[:, at] + total


def kernel(
    x_hbm, bin_hbm, valid_hbm, stack_hbm, high_hbm, low_hbm, fine_hbm, out_ref,
    x, bin_ref, valid_ref, stack_ref, send, recv, key_send, keys, real, imag, reals, imags, sums, gathered,
    high, low, fine, load_sem, table_sem, send_sem, key_send_sem, recv_sem, key_sem, row_send_sem, row_sem,
):
    me = lax.axis_index("stn")
    band = lax.axis_index("frq")
    my_group = me // GROUP
    my_x, my_z, my_w = me // 16, me // 4 % 4, me % 4
    gathers = my_z < 2
    my_chunk = my_x * 8 + my_z * 4 + my_w
    units = pltpu.ACC(0), pltpu.ACC(1)

    load = pltpu.make_async_copy(x_hbm, x, load_sem)
    load.start()
    table_copies = [
        pltpu.make_async_copy(high_hbm, high, table_sem.at[0]),
        pltpu.make_async_copy(low_hbm, low, table_sem.at[1]),
        pltpu.make_async_copy(fine_hbm.at[band], fine, table_sem.at[2]),
        pltpu.make_async_copy(stack_hbm, stack_ref, table_sem.at[3]),
    ]
    bin_load = pltpu.make_async_copy(bin_hbm, bin_ref, table_sem.at[4])
    bin_load.start()
    valid_load = pltpu.make_async_copy(valid_hbm, valid_ref, table_sem.at[5])
    valid_load.start()

    barrier = pltpu.get_barrier_semaphore()
    pl.semaphore_signal(barrier, inc=1, device_id=(me, 1 - band), device_id_type=MESH)

    @pl.when(gathers)
    def _():
        for x_off in FAR_FIRST:

            def greet(step, carry, x_off=x_off):
                to = (my_x + x_off) % 4 * 16 + (my_z + 2 + step // 4) % 4 * 4 + (my_w + step) % 4
                pl.semaphore_signal(barrier, inc=1, device_id=(to, band), device_id_type=MESH)
                return carry

            lax.fori_loop(0, 16 if x_off else 8, greet, 0)
        for z_off in (1, 0):

            def greet_near(step, carry, z_off=z_off):
                to = my_x * 16 + (my_z + z_off) % 4 * 4 + (my_w + step) % 4
                pl.semaphore_signal(barrier, inc=1, device_id=(to, band), device_id_type=MESH)
                return carry

            lax.fori_loop(0 if z_off else 1, GROUP, greet_near, 0)

    for copy in table_copies:
        copy.start()
    load.wait()
    pl.run_scoped(
        lambda *accs: whiten_own(x, send, accs), *(unit((4 * STN, 2 * LANES), jnp.float32) for unit in units)
    )
    bin_load.wait()
    valid_load.wait()
    own_key = jnp.where(valid_ref[...] > 0, bin_ref[...], BINS)
    key_send[...] = own_key

    @pl.when(gathers)
    def _():
        keys[me] = own_key
        recv[me] = send[my_chunk]
        pl.semaphore_wait(barrier, CHUNKS)

    @pl.when(jnp.logical_not(gathers))
    def _():
        pl.semaphore_wait(barrier, CHUNKS + 1)

    for x_off in FAR_FIRST:

        def post(step, carry, x_off=x_off):
            to_x, to_z, to_w = (my_x + x_off) % 4, step // 4, (my_w + step) % 4
            to = to_x * 16 + to_z * 4 + to_w

            def start():
                pltpu.make_async_remote_copy(
                    src_ref=send.at[to_x * 8 + to_z * 4 + to_w],
                    dst_ref=recv.at[me],
                    send_sem=send_sem,
                    recv_sem=recv_sem.at[my_group],
                    device_id=(to, band),
                    device_id_type=MESH,
                ).start()
                pltpu.make_async_remote_copy(
                    src_ref=key_send,
                    dst_ref=keys.at[me],
                    send_sem=key_send_sem,
                    recv_sem=key_sem.at[my_group],
                    device_id=(to, band),
                    device_id_type=MESH,
                ).start()

            if x_off:
                start()
            else:
                pl.when(to != me)(start)
            return carry

        lax.fori_loop(0, 8, post, 0)

    def await_all(ref, count, sem):
        some = ref.at[pl.ds(0, count)]
        pltpu.make_async_copy(some, some, sem).wait()

    def await_group(group, count):
        await_all(recv, count, recv_sem.at[group])
        await_all(keys, count, key_sem.at[group])

    def plan(step):
        early = step < 9
        side = (step + 1) // 2
        even = step % 2 == 0
        target = jnp.where(early, jnp.where(even, GROUPS - side, side), step - 4)
        needed = jnp.where(early, jnp.where(even, GROUPS - side - 1, side), step - 4)
        return (my_group + target) % GROUPS, (my_group + needed) % GROUPS

    def correlate(*halves):
        unpack_group, bin_group, binned = binning(recv, keys, real, imag, reals, imags, halves)
        await_group(my_group, GROUP - 1)
        unpack_group(my_group)
        needed = plan(0)[1]
        await_group(needed, GROUP)
        unpack_group(needed)

        def advance(step, carry):
            target, needed = plan(step - 1)[0], plan(step)[1]
            await_group(needed, GROUP)
            bin_group(target)
            unpack_group(needed)
            return carry

        lax.fori_loop(1, GROUPS - 1, advance, 0)
        bin_group(plan(GROUPS - 2)[0])
        bin_group(plan(GROUPS - 1)[0])
        sums[...] = binned().reshape(BINS, 1, 2 * LANES)

    slot = band * CHUNKS + my_chunk

    @pl.when(gathers)
    def _():
        pl.run_scoped(correlate, *(unit((BINS, 2 * LANES), jnp.float32) for unit in units))
        gathered[slot] = sums[me]

        def deliver(step, carry):
            to = step // 8 % 4 * 16 + step // 32 * 4 + step % 4
            there = step // 4 % 2

            @pl.when(jnp.logical_or(to != me, there != band))
            def _():
                pltpu.make_async_remote_copy(
                    src_ref=sums.at[to],
                    dst_ref=gathered.at[slot],
                    send_sem=row_send_sem,
                    recv_sem=row_sem,
                    device_id=(to, there),
                    device_id_type=MESH,
                ).start()

            return carry

        lax.fori_loop(0, N_STN * N_FRQ, deliver, 0)

    for copy in table_copies:
        copy.wait()

    def finish(*accs):
        push_tables(high, low, accs)

        @pl.when(gathers)
        def _():
            await_all(gathered, SLOTS - 1, row_sem)

        @pl.when(jnp.logical_not(gathers))
        def _():
            await_all(gathered, SLOTS, row_sem)

        transform(gathered, fine, stack_ref, out_ref, accs)

    pl.run_scoped(finish, *(unit((LANES, 2 * LANES), jnp.float32) for unit in units))

    @pl.when(gathers)
    def _():
        await_all(send, CHUNKS - 1, send_sem)
        await_all(keys, CHUNKS - 1, key_send_sem)
        await_all(gathered, SLOTS - 1, row_send_sem)
        await_all(gathered, SLOTS, row_send_sem)

    @pl.when(jnp.logical_not(gathers))
    def _():
        await_all(send, CHUNKS, send_sem)
        await_all(keys, CHUNKS, key_send_sem)


def local(spectra, pair_bin, pair_valid, stack_in):
    high, low, fine = tables()
    block = (N_STN, STN, LANES)
    twin = (N_STN, 2 * STN, LANES)
    return pl.pallas_call(
        kernel,
        out_shape=jax.ShapeDtypeStruct((1, HALF), jnp.float32),
        in_specs=[pl.BlockSpec(memory_space=pltpu.HBM)] * 7,
        out_specs=pl.BlockSpec(memory_space=pltpu.VMEM),
        scratch_shapes=[
            pltpu.VMEM((STN, 2, BAND), jnp.bfloat16),
            pltpu.VMEM((ROWS, LANES), jnp.int32),
            pltpu.VMEM((ROWS, LANES), jnp.int32),
            pltpu.VMEM((1, HALF), jnp.float32),
            pltpu.VMEM((CHUNKS, 2 * STN, LANES), jnp.bfloat16),
            pltpu.VMEM(twin, jnp.bfloat16),
            pltpu.VMEM((ROWS, LANES), jnp.int32),
            pltpu.VMEM((N_STN, ROWS, LANES), jnp.int32),
            pltpu.VMEM(block, jnp.float32),
            pltpu.VMEM(block, jnp.float32),
            pltpu.VMEM(twin, jnp.bfloat16),
            pltpu.VMEM(twin, jnp.bfloat16),
            pltpu.VMEM((BINS, 1, 2 * LANES), jnp.float32),
            pltpu.VMEM((SLOTS, 1, 2 * LANES), jnp.float32),
            pltpu.VMEM(high.shape, jnp.bfloat16),
            pltpu.VMEM(low.shape, jnp.bfloat16),
            pltpu.VMEM(fine.shape[1:], jnp.float32),
            pltpu.SemaphoreType.DMA,
            pltpu.SemaphoreType.DMA((6,)),
            pltpu.SemaphoreType.DMA,
            pltpu.SemaphoreType.DMA,
            pltpu.SemaphoreType.DMA((GROUPS,)),
            pltpu.SemaphoreType.DMA((GROUPS,)),
            pltpu.SemaphoreType.DMA,
            pltpu.SemaphoreType.DMA,
        ],
        compiler_params=pltpu.CompilerParams(
            collective_id=0, has_side_effects=True, vmem_limit_bytes=32 * 2**20
        ),
    )(
        *(
            pltpu.with_memory_space_constraint(operand, pltpu.HBM)
            for operand in (
                spectra,
                pair_bin.reshape(ROWS, LANES),
                pair_valid.reshape(ROWS, LANES),
                stack_in,
                jnp.asarray(high),
                jnp.asarray(low),
                jnp.asarray(fine),
            )
        )
    )


def solution(mesh):
    placed = (P("stn", None, "frq"), P("stn", None), P("stn"), P("stn", "frq"))
    return jax.shard_map(
        local, mesh=mesh, in_specs=placed, out_specs=P("stn", "frq"), check_vma=False
    )
```

time: 24.6 us -> 23.5 us (0.955)
  the two profiles are of different devices: /device:TPU:1 before, /device:TPU:97 now
where the time goes in v3:
time: 23.5 us; the launch traced here: 23.4 us
  Pallas kernels  22.8 us (97%)
  local copies, waits for them, and re-layouts  0.6 us (3%)
    pallas_call x1, Pallas kernels, local(): pl.pallas_call(kernel, out_shape=jax.ShapeDtypeStruct((1, HALF), jnp.floa...  22.8 us
    unnamed x1, local copies, waits for them, and re-layouts  0.6 us

profile of v3, /device:TPU:97, one launch (start us, length us, event | category | flops | bytes accessed | tf_op | source)
XLA Modules:
  0.0 23.4 jit_solution(7472251192755198774)
XLA Ops:
  0.0 22.8 %shard_map.73 = f32[1,1024]{1,0:T(1,128)S(1)} custom-call(bf16[8,2,4096]{2,1,0:T(2,128)(2,1)} %x_hbm.1, s32[2,128]{1,0:T(2,128)} %bitcast.2, s32[2,128]{1,0:T(2,128)} %bitcast.3, f32[1,1024]{1,0:T(1,128)} %stack_hbm.1, bf16[256,256]{1,0:T(8,128)(2,1)} %constant.6.clone.high_hbm, bf16[256,256]{1,0:T(8,128)(2,1)} %constant.7.clone.low_hbm, ...), custom_call_target="tpu_custom_call" | custom-call | tf_op jit(solution)/shard_map/pallas_call | solution.py:374
  22.8 0.6 %copy.9 = f32[1,1024]{1,0:T(1,128)} copy(f32[1,1024]{1,0:T(1,128)S(1)} %shard_map.73) | data formatting | bytes 8192

commit v4 on v3

--- a/solution.py
+++ b/solution.py
@@ -28,7 +28,7 @@
 PERIOD = SAMPLES // LANES
 PAIRS_DEV = ROUNDS * STN * STN
 ROWS = PAIRS_DEV // LANES
-FAR_FIRST = (2, 1, 3, 0)
+FAR_FIRST = (0, 1, 3, 2)
 MESH = pl.DeviceIdType.MESH
 
 
@@ -95,14 +95,15 @@
     lax.fori_loop(1, CHUNKS // wide // len(accs), again, 0)
 
 
-def binning(recv, keys, real, imag, reals, imags, halves):
-    bin_row = lax.broadcasted_iota(jnp.int32, (BINS, LANES), 0)
+def binning(recv, keys, wide_keys, real, imag, reals, imags, halves):
+    bin_row = lax.broadcasted_iota(jnp.int32, (BINS, LANES), 0).astype(jnp.float32)
 
     def unpack_group(group):
         for part in range(GROUP):
             block = group * GROUP + part
             white = recv[block].astype(jnp.float32)
             re, im = white[:STN], white[STN:]
+            wide_keys[block] = keys[block].astype(jnp.float32)
             real[block] = re
             imag[block] = im
             reals[block] = twice(re, re)
@@ -128,7 +129,7 @@
     def onehot_of(block):
         return jnp.concatenate(
             [
-                jnp.where(keys[block, pl.ds(row, 1), :] == bin_row, 1.0, 0.0).astype(jnp.bfloat16)
+                jnp.where(wide_keys[block, pl.ds(row, 1), :] == bin_row, 1.0, 0.0).astype(jnp.bfloat16)
                 for row in range(ROWS)
             ],
             axis=1,
@@ -175,7 +176,7 @@
 
 def kernel(
     x_hbm, bin_hbm, valid_hbm, stack_hbm, high_hbm, low_hbm, fine_hbm, out_ref,
-    x, bin_ref, valid_ref, stack_ref, send, recv, key_send, keys, real, imag, reals, imags, sums, gathered,
+    x, bin_ref, valid_ref, stack_ref, send, recv, key_send, keys, wide_keys, real, imag, reals, imags, sums, gathered,
     high, low, fine, load_sem, table_sem, send_sem, key_send_sem, recv_sem, key_sem, row_send_sem, row_sem,
 ):
     me = lax.axis_index("stn")
@@ -185,6 +186,28 @@
     gathers = my_z < 2
     my_chunk = my_x * 8 + my_z * 4 + my_w
     units = pltpu.ACC(0), pltpu.ACC(1)
+
+    barrier = pltpu.get_barrier_semaphore()
+    pl.semaphore_signal(barrier, inc=1, device_id=(me, 1 - band), device_id_type=MESH)
+
+    @pl.when(gathers)
+    def _():
+        for x_off in (2, 1, 3, 0):
+
+            def greet(step, carry, x_off=x_off):
+                to = (my_x + x_off) % 4 * 16 + (my_z + 2 + step // 4) % 4 * 4 + (my_w + step) % 4
+                pl.semaphore_signal(barrier, inc=1, device_id=(to, band), device_id_type=MESH)
+                return carry
+
+            lax.fori_loop(0, 16 if x_off else 8, greet, 0, unroll=True)
+        for z_off in (1, 0):
+
+            def greet_near(step, carry, z_off=z_off):
+                to = my_x * 16 + (my_z + z_off) % 4 * 4 + (my_w + step) % 4
+                pl.semaphore_signal(barrier, inc=1, device_id=(to, band), device_id_type=MESH)
+                return carry
+
+            lax.fori_loop(0 if z_off else 1, GROUP, greet_near, 0)
 
     load = pltpu.make_async_copy(x_hbm, x, load_sem)
     load.start()
@@ -199,28 +222,6 @@
     valid_load = pltpu.make_async_copy(valid_hbm, valid_ref, table_sem.at[5])
     valid_load.start()
 
-    barrier = pltpu.get_barrier_semaphore()
-    pl.semaphore_signal(barrier, inc=1, device_id=(me, 1 - band), device_id_type=MESH)
-
-    @pl.when(gathers)
-    def _():
-        for x_off in FAR_FIRST:
-
-            def greet(step, carry, x_off=x_off):
-                to = (my_x + x_off) % 4 * 16 + (my_z + 2 + step // 4) % 4 * 4 + (my_w + step) % 4
-                pl.semaphore_signal(barrier, inc=1, device_id=(to, band), device_id_type=MESH)
-                return carry
-
-            lax.fori_loop(0, 16 if x_off else 8, greet, 0)
-        for z_off in (1, 0):
-
-            def greet_near(step, carry, z_off=z_off):
-                to = my_x * 16 + (my_z + z_off) % 4 * 4 + (my_w + step) % 4
-                pl.semaphore_signal(barrier, inc=1, device_id=(to, band), device_id_type=MESH)
-                return carry
-
-            lax.fori_loop(0 if z_off else 1, GROUP, greet_near, 0)
-
     for copy in table_copies:
         copy.start()
     load.wait()
@@ -229,7 +230,7 @@
     )
     bin_load.wait()
     valid_load.wait()
-    own_key = jnp.where(valid_ref[...] > 0, bin_ref[...], BINS)
+    own_key = jnp.where(valid_ref[...] > 0, bin_ref[...], BINS).astype(jnp.float32).astype(jnp.bfloat16)
     key_send[...] = own_key
 
     @pl.when(gathers)
@@ -272,7 +273,7 @@
                 pl.when(to != me)(start)
             return carry
 
-        lax.fori_loop(0, 8, post, 0)
+        lax.fori_loop(0, 8, post, 0, unroll=True)
 
     def await_all(ref, count, sem):
         some = ref.at[pl.ds(0, count)]
@@ -291,7 +292,7 @@
         return (my_group + target) % GROUPS, (my_group + needed) % GROUPS
 
     def correlate(*halves):
-        unpack_group, bin_group, binned = binning(recv, keys, real, imag, reals, imags, halves)
+        unpack_group, bin_group, binned = binning(recv, keys, wide_keys, real, imag, reals, imags, halves)
         await_group(my_group, GROUP - 1)
         unpack_group(my_group)
         needed = plan(0)[1]
@@ -317,24 +318,28 @@
         pl.run_scoped(correlate, *(unit((BINS, 2 * LANES), jnp.float32) for unit in units))
         gathered[slot] = sums[me]
 
-        def deliver(step, carry):
-            to = step // 8 % 4 * 16 + step // 32 * 4 + step % 4
-            there = step // 4 % 2
-
-            @pl.when(jnp.logical_or(to != me, there != band))
-            def _():
-                pltpu.make_async_remote_copy(
-                    src_ref=sums.at[to],
-                    dst_ref=gathered.at[slot],
-                    send_sem=row_send_sem,
-                    recv_sem=row_sem,
-                    device_id=(to, there),
-                    device_id_type=MESH,
-                ).start()
-
-            return carry
-
-        lax.fori_loop(0, N_STN * N_FRQ, deliver, 0)
+        for there in range(N_FRQ):
+            for y_low in range(2):
+                for z_at in range(4):
+                    base = z_at * 4 + y_low * 2
+
+                    def deliver(step, carry, base=base, there=there):
+                        to = step // 2 * 16 + base + step % 2
+
+                        @pl.when(jnp.logical_or(to != me, there != band))
+                        def _():
+                            pltpu.make_async_remote_copy(
+                                src_ref=sums.at[to],
+                                dst_ref=gathered.at[slot],
+                                send_sem=row_send_sem,
+                                recv_sem=row_sem,
+                                device_id=(to, there),
+                                device_id_type=MESH,
+                            ).start()
+
+                        return carry
+
+                    lax.fori_loop(0, 8, deliver, 0, unroll=True)
 
     for copy in table_copies:
         copy.wait()
@@ -383,8 +388,9 @@
             pltpu.VMEM((1, HALF), jnp.float32),
             pltpu.VMEM((CHUNKS, 2 * STN, LANES), jnp.bfloat16),
             pltpu.VMEM(twin, jnp.bfloat16),
-            pltpu.VMEM((ROWS, LANES), jnp.int32),
-            pltpu.VMEM((N_STN, ROWS, LANES), jnp.int32),
+            pltpu.VMEM((ROWS, LANES), jnp.bfloat16),
+            pltpu.VMEM((N_STN, ROWS, LANES), jnp.bfloat16),
+            pltpu.VMEM((N_STN, ROWS, LANES), jnp.float32),
             pltpu.VMEM(block, jnp.float32),
             pltpu.VMEM(block, jnp.float32),
             pltpu.VMEM(twin, jnp.bfloat16),

time: 23.5 us -> 21.3 us (0.906)
  the two profiles are of different devices: /device:TPU:97 before, /device:TPU:1 now
where the time goes in v4:
time: 21.3 us; the launch traced here: 21.1 us
  Pallas kernels  20.5 us (96%)
  local copies, waits for them, and re-layouts  0.6 us (3%)
    pallas_call x1, Pallas kernels, local(): pl.pallas_call(kernel, out_shape=jax.ShapeDtypeStruct((1, HALF), jnp.floa...  20.5 us
    unnamed x1, local copies, waits for them, and re-layouts  0.6 us

profile of v4, /device:TPU:1, one launch (start us, length us, event | category | flops | bytes accessed | tf_op | source)
XLA Modules:
  0.0 21.1 jit_solution(3848005245999942862)
XLA Ops:
  0.0 20.5 %shard_map.73 = f32[1,1024]{1,0:T(1,128)S(1)} custom-call(bf16[8,2,4096]{2,1,0:T(2,128)(2,1)} %x_hbm.1, s32[2,128]{1,0:T(2,128)} %bitcast.2, s32[2,128]{1,0:T(2,128)} %bitcast.3, f32[1,1024]{1,0:T(1,128)} %stack_hbm.1, bf16[256,256]{1,0:T(8,128)(2,1)} %constant.6.clone.high_hbm, bf16[256,256]{1,0:T(8,128)(2,1)} %constant.7.clone.low_hbm, ...), custom_call_target="tpu_custom_call" | custom-call | tf_op jit(solution)/shard_map/pallas_call | solution.py:379
  20.5 0.6 %copy.9 = f32[1,1024]{1,0:T(1,128)} copy(f32[1,1024]{1,0:T(1,128)S(1)} %shard_map.73) | data formatting | bytes 8192

commit v5 on v4

--- a/solution.py
+++ b/solution.py
@@ -167,10 +167,8 @@
     mixed = [pltpu.matmul_pop(acc) for acc in accs]
     for part in range(HALF // PERIOD):
         at = pl.ds(part * PERIOD, PERIOD)
-        total = sum(
-            jnp.sum(one * fine[pl.ds(unit * LANES, LANES), at], axis=0, keepdims=True)
-            for unit, one in enumerate(mixed)
-        )
+        products = [one * fine[pl.ds(unit * LANES, LANES), at] for unit, one in enumerate(mixed)]
+        total = jnp.sum(products[0] + products[1], axis=0, keepdims=True)
         out_ref[:, at] = stack_ref[:, at] + total
 
 
@@ -207,7 +205,7 @@
                 pl.semaphore_signal(barrier, inc=1, device_id=(to, band), device_id_type=MESH)
                 return carry
 
-            lax.fori_loop(0 if z_off else 1, GROUP, greet_near, 0)
+            lax.fori_loop(0 if z_off else 1, GROUP, greet_near, 0, unroll=True)
 
     load = pltpu.make_async_copy(x_hbm, x, load_sem)
     load.start()
@@ -344,21 +342,6 @@
     for copy in table_copies:
         copy.wait()
 
-    def finish(*accs):
-        push_tables(high, low, accs)
-
-        @pl.when(gathers)
-        def _():
-            await_all(gathered, SLOTS - 1, row_sem)
-
-        @pl.when(jnp.logical_not(gathers))
-        def _():
-            await_all(gathered, SLOTS, row_sem)
-
-        transform(gathered, fine, stack_ref, out_ref, accs)
-
-    pl.run_scoped(finish, *(unit((LANES, 2 * LANES), jnp.float32) for unit in units))
-
     @pl.when(gathers)
     def _():
         await_all(send, CHUNKS - 1, send_sem)
@@ -370,6 +353,21 @@
     def _():
         await_all(send, CHUNKS, send_sem)
         await_all(keys, CHUNKS, key_send_sem)
+
+    def finish(*accs):
+        push_tables(high, low, accs)
+
+        @pl.when(gathers)
+        def _():
+            await_all(gathered, SLOTS - 1, row_sem)
+
+        @pl.when(jnp.logical_not(gathers))
+        def _():
+            await_all(gathered, SLOTS, row_sem)
+
+        transform(gathered, fine, stack_ref, out_ref, accs)
+
+    pl.run_scoped(finish, *(unit((LANES, 2 * LANES), jnp.float32) for unit in units))
 
 
 def local(spectra, pair_bin, pair_valid, stack_in):

time: 21.3 us -> 21.3 us (level)
  no operation moved by 1% of the time
where the time goes in v5:
time: 21.3 us; the launch traced here: 21.1 us
  Pallas kernels  20.5 us (96%)
  local copies, waits for them, and re-layouts  0.6 us (3%)
    pallas_call x1, Pallas kernels, local(): pl.pallas_call(kernel, out_shape=jax.ShapeDtypeStruct((1, HALF), jnp.floa...  20.5 us
    unnamed x1, local copies, waits for them, and re-layouts  0.6 us

profile of v5, /device:TPU:1, one launch (start us, length us, event | category | flops | bytes accessed | tf_op | source)
XLA Modules:
  0.0 21.1 jit_solution(8471175449480138760)
XLA Ops:
  0.0 20.5 %shard_map.73 = f32[1,1024]{1,0:T(1,128)S(1)} custom-call(bf16[8,2,4096]{2,1,0:T(2,128)(2,1)} %x_hbm.1, s32[2,128]{1,0:T(2,128)} %bitcast.2, s32[2,128]{1,0:T(2,128)} %bitcast.3, f32[1,1024]{1,0:T(1,128)} %stack_hbm.1, bf16[256,256]{1,0:T(8,128)(2,1)} %constant.6.clone.high_hbm, bf16[256,256]{1,0:T(8,128)(2,1)} %constant.7.clone.low_hbm, ...), custom_call_target="tpu_custom_call" | custom-call | tf_op jit(solution)/shard_map/pallas_call | solution.py:377
  20.5 0.6 %copy.9 = f32[1,1024]{1,0:T(1,128)} copy(f32[1,1024]{1,0:T(1,128)S(1)} %shard_map.73) | data formatting | bytes 8192
